TPU v7x, 512 devices: a whole 4x4x16 slice. The times are simulated.
512 devices in a mesh: loop: 64 (over y_lo, z, core), grp: 8 (over x, y_hi).
Axes of the slice: x: 4, y: 4 (y_hi: 2, y_lo: 2; y = y_hi * 2 + y_lo), z: 16, core: 2. Of those that a mesh axis runs over, the one named last changes fastest.
Arguments:
- ratings: bfloat16 [2, 262144, 2048], P(None, ('loop', 'grp')), may hold values from -2.5 to 2.5, as said below
- user_factors: float32 [262144, 128], P(('loop', 'grp')), may hold values from -2 to 2
- user_accum: float32 [262144, 128], P(('loop', 'grp')), may hold values from 20 to 400
- item_factors: float32 [131072, 128], P('loop'), may hold values from -2 to 2
- item_accum: float32 [131072, 128], P('loop'), may hold values from 20 to 400
Outputs:
- users_out: float32 [262144, 128], P(('loop', 'grp'))
- items_out: float32 [131072, 128], P('loop')
Inputs may be any that keep to these rules, and one draw needn't show every extreme that they name: `ratings`: each entry is 0 (unobserved) or has magnitude 0.5 or more.
All inputs are finite; a program needn't handle non-finite values.
Results may differ from a plain program's by a relative error of at most 0.0085.
Values may be sent and summed in bfloat16 or wider, within the bound.
A program may use at most 64 MiB of HBM per device.

v0:
```python
import jax
import jax.numpy as jnp
from jax import lax
from jax.sharding import PartitionSpec as P

SUB = 2
INNER = 2


shrink = 0.05
learn_rate = 0.2
tiny_eps = 1e-06


def shifted(shard, axis, by):
    devices = lax.axis_size(axis)
    return lax.ppermute(shard, axis, [(i, (i + by) % devices) for i in range(devices)])


def adagrad(param, accum, grad):
    accum = accum + grad * grad
    return (param - learn_rate * grad / jnp.sqrt(accum + tiny_eps), accum)


def residual_terms(rate_full, observed, users, item_half):
    user_half = users.astype(jnp.bfloat16)
    predicted = lax.dot_general(
        user_half, item_half, (((1,), (1,)), ((), ())), preferred_element_type=jnp.float32
    )
    resid = (observed * (rate_full - predicted)).astype(jnp.bfloat16)
    grad_user = -jnp.dot(resid, item_half, preferred_element_type=jnp.float32) + shrink * users
    return (user_half, resid, grad_user)


def local(ratings, user_factors, user_accum, item_factors, item_accum):
    users = user_factors
    user_acc = user_accum
    items = item_factors
    item_acc = item_accum
    for sub_epoch in range(SUB):
        if sub_epoch > 0:
            items, item_acc = shifted((items, item_acc), "loop", 1)
        rate_full = ratings[sub_epoch].astype(jnp.float32)
        observed = (jnp.abs(rate_full) > 0.25).astype(jnp.float32)
        for inner_step in range(INNER):
            item_half = items.astype(jnp.bfloat16)
            user_half, resid, grad_user = residual_terms(rate_full, observed, users, item_half)
            own_term = -lax.dot_general(
                resid, user_half, (((0,), (0,)), ((), ())), preferred_element_type=jnp.float32
            )
            grad_item = (
                lax.psum(own_term.astype(jnp.bfloat16), "grp").astype(jnp.float32) + shrink * items
            )
            users, user_acc = adagrad(users, user_acc, grad_user)
            items, item_acc = adagrad(items, item_acc, grad_item)
    return (users, items)


def solution(mesh):
    in_specs = (
        P(None, ("loop", "grp"), None),
        P(("loop", "grp"), None),
        P(("loop", "grp"), None),
        P("loop", None),
        P("loop", None),
    )
    out_specs = (P(("loop", "grp"), None), P("loop", None))
    return jax.shard_map(local, mesh=mesh, in_specs=in_specs, out_specs=out_specs, check_vma=False)
```

profile of v0, /device:TPU:64, one launch (start us, length us, event | category | flops | bytes accessed | tf_op | source)
XLA Modules:
  0.0 459.1 jit_solution(7370954499293579164)
XLA Ops:
  7.2 0.0 all-reduce.5.cloned.1.call-start
  7.2 0.0 copy-start.6
  7.2 3.0 fusion.2
  10.3 1.6 fusion.10
  11.8 0.0 all-reduce.5.cloned.1.call-update
  11.9 0.0 all-reduce.7.cloned.1.call-start
  11.9 2.5 multiply_subtract_fusion.7
  14.4 102.7 %all-reduce.5.cloned.1.call-done = bf16[2048,128]{1,0:T(8,128)(2,1)} async-done(((bf16[2048,128]{1,0:T(8,128)(2,1)}), bf16[2048,128]{1,0:T(8,128)(2,1)}) %all-reduce.5.cloned.1.call-update) | async-done | bytes 524304 | tf_op jit(solution)/shard_map/psum | solution.py:52
  117.1 3.4 fusion.4
  120.5 1.6 fusion.11
  122.1 0.0 all-reduce.7.cloned.1.call-update
  122.1 0.0 all-reduce.9.cloned.1.call-start
  122.2 99.3 %all-reduce.7.cloned.1.call-done = bf16[2048,128]{1,0:T(8,128)(2,1)} async-done(((bf16[2048,128]{1,0:T(8,128)(2,1)}), bf16[2048,128]{1,0:T(8,128)(2,1)}) %all-reduce.7.cloned.1.call-update) | async-done | bytes 524304 | tf_op jit(solution)/shard_map/psum | solution.py:52
  221.4 3.3 multiply_add_fusion.2
  224.8 1.9 collective-permute-start
  226.7 2.8 multiply_subtract_fusion.6
  229.5 3.6 collective-permute-start.1
  233.1 7.8 %collective-permute-done = f32[2048,128]{1,0:T(8,128)S(1)} collective-permute-done((f32[2048,128]{1,0:T(8,128)S(1)}, f32[2048,128]{1,0:T(8,128)S(1)}, u32[]{:S(2)}, u32[]{:S(2)}) %collective-permute-start) | collective-permute-done | bytes 1048608 | tf_op jit(solution)/shard_map/ppermute | solution.py:17
  240.9 1.1 fusion.7
  241.9 1.6 fusion.12
  243.5 0.0 all-reduce.9.cloned.1.call-update
  243.5 0.2 all-reduce.11.cloned.1.call-start
  243.8 2.4 fusion.25
  246.1 6.1 %collective-permute-done.1 = f32[2048,128]{1,0:T(8,128)} collective-permute-done((f32[2048,128]{1,0:T(8,128)}, f32[2048,128]{1,0:T(8,128)}, u32[]{:S(2)}, u32[]{:S(2)}) %collective-permute-start.1) | collective-permute-done | bytes 1048608 | tf_op jit(solution)/shard_map/ppermute | solution.py:17
  252.2 91.8 %all-reduce.9.cloned.1.call-done = bf16[2048,128]{1,0:T(8,128)(2,1)} async-done(((bf16[2048,128]{1,0:T(8,128)(2,1)}), bf16[2048,128]{1,0:T(8,128)(2,1)}) %all-reduce.9.cloned.1.call-update) | async-done | bytes 524304 | tf_op jit(solution)/shard_map/psum | solution.py:52
  344.0 1.7 fusion.18
  345.8 2.7 fusion.9
  348.5 1.6 fusion.13
  350.1 0.0 all-reduce.11.cloned.1.call-update
  350.1 2.6 multiply_subtract_fusion.4
  352.7 96.6 %all-reduce.11.cloned.1.call-done = bf16[2048,128]{1,0:T(8,128)(2,1)} async-done(((bf16[2048,128]{1,0:T(8,128)(2,1)}), bf16[2048,128]{1,0:T(8,128)(2,1)}) %all-reduce.11.cloned.1.call-update) | async-done | bytes 524304 | tf_op jit(solution)/shard_map/psum | solution.py:52
  449.4 3.2 multiply_subtract_fusion
  (17 shorter events, 0.0 us)
Async XLA Ops:
  7.2 109.9 %all-reduce.5.cloned.1.call-start = ((), (), s32[]{:S(2)}) async-start(), calls=%async_computation | async-start | bytes 1048576 | tf_op jit(solution)/shard_map/psum | solution.py:52
  7.2 3.0 copy-start.6
  10.3 1.7 copy-start
  10.3 1.7 copy-start.5
  11.9 209.6 %all-reduce.7.cloned.1.call-start = ((), (), s32[]{:S(2)}) async-start(), calls=%async_computation.1 | async-start | bytes 1048576 | tf_op jit(solution)/shard_map/psum | solution.py:52
  117.1 3.4 copy-start.3
  122.1 221.9 %all-reduce.9.cloned.1.call-start = ((), (), s32[]{:S(2)}) async-start(), calls=%async_computation.2 | async-start | bytes 1048576 | tf_op jit(solution)/shard_map/psum | solution.py:52
  221.4 5.2 %copy-start.1 = (f32[2048,128]{1,0:T(8,128)S(1)}, f32[2048,128]{1,0:T(8,128)}, u32[]{:S(2)}) copy-start(f32[2048,128]{1,0:T(8,128)} %param.8) | copy-start | bytes 3145732
  221.4 5.2 %copy-start.2 = (f32[2048,128]{1,0:T(8,128)S(1)}, f32[2048,128]{1,0:T(8,128)}, u32[]{:S(2)}) copy-start(f32[2048,128]{1,0:T(8,128)} %param.9) | copy-start | bytes 3145732
  221.4 5.3 %copy-start.4 = (bf16[2048,128]{1,0:T(8,128)(2,1)S(1)}, bf16[2048,128]{1,0:T(8,128)(2,1)}, u32[]{:S(2)}) copy-start(bf16[2048,128]{1,0:T(8,128)(2,1)} %all-reduce.5.cloned.1.call-done) | copy-start | bytes 1572868
  224.8 16.1 %collective-permute-start = (f32[2048,128]{1,0:T(8,128)S(1)}, f32[2048,128]{1,0:T(8,128)S(1)}, u32[]{:S(2)}, u32[]{:S(2)}) collective-permute-start(f32[2048,128]{1,0:T(8,128)S(1)} %get-tuple-element.5), channel_id=1, source_target_pairs={{0,8},{8,16},{16,24},{24,32},{32,40},{40,48},{48,56},{56,64},{64,7... | collective-permute-start | bytes 3145736 | tf_op jit(solution)/shard_map/ppermute | solution.py:17
  226.7 14.2 %copy-start.8 = (bf16[2,512,2048]{2,1,0:T(8,128)(2,1)S(1)}, bf16[2,512,2048]{2,1,0:T(8,128)(2,1)}, u32[]{:S(2)}) copy-start(bf16[2,512,2048]{2,1,0:T(8,128)(2,1)} %param.5) | copy-start | bytes 12582916
  229.5 22.7 %collective-permute-start.1 = (f32[2048,128]{1,0:T(8,128)}, f32[2048,128]{1,0:T(8,128)}, u32[]{:S(2)}, u32[]{:S(2)}) collective-permute-start(f32[2048,128]{1,0:T(8,128)} %get-tuple-element.4), channel_id=1, source_target_pairs={{0,8},{8,16},{16,24},{24,32},{32,40},{40,48},{48,56},{56,64},{64,7... | collective-permute-start | bytes 3145736 | tf_op jit(solution)/shard_map/ppermute | solution.py:17
  243.5 205.8 %all-reduce.11.cloned.1.call-start = ((), (), s32[]{:S(2)}) async-start(), calls=%async_computation.3 | async-start | bytes 1048576 | tf_op jit(solution)/shard_map/psum | solution.py:52
  345.7 2.7 copy-start.7
Sparse Core Ops, SparseCore 0:
  12.0 105.0 all-reduce.4
  122.2 99.1 all-reduce.6
  243.7 100.2 all-reduce.8
  350.2 99.0 all-reduce.10
where the time goes:
time: 460 us; the launch traced here: 459 us
  waiting for transfers between devices  404 us (88%)
  matrix products  26.7 us (6%)
  between operations  13.9 us (3%)
  other arithmetic  8.22 us (2%)
  starting transfers between devices  5.81 us (1%)
    psum x4, waiting for transfers between devices, local(): lax.psum(own_term.astype(jnp.bfloat16), 'grp').astype(jnp.float32)  390 us
    ppermute x2, waiting for transfers between devices, shifted(): lax.ppermute(shard, axis, [(i, (i + by) % devices) for i in range(devices)])  13.8 us
    dot_general x4, matrix products, residual_terms(): jnp.dot(resid, item_half, preferred_element_type=jnp.float32)  10.3 us
    dot_general x4, matrix products, residual_terms(): lax.dot_general(user_half, item_half, (((1,), (1,)), ((), ())), preferred...  10.2 us
  transfers between devices with their start and end apart: 6, of which 6 were waited for; matrix products, arithmetic and copies ran while one was open for 3% of the time, Pallas kernels for 0%

commit v1 on v0

v1 whole, which is shorter than its diff:
```python
import functools

import jax
import jax.numpy as jnp
from jax import lax
from jax.experimental import pallas as pl
from jax.experimental.pallas import tpu as pltpu
from jax.sharding import PartitionSpec as P

SUB = 2
INNER = 2
STEPS = SUB * INNER

shrink = 0.05
learn_rate = 0.2
tiny_eps = 1e-06

NC = 2
MESH = pl.DeviceIdType.MESH


def adagrad(param, accum, grad):
    accum = accum + grad * grad
    return param - learn_rate * grad / jnp.sqrt(accum + tiny_eps), accum


def kernel(
    n_loop, n_grp,
    ratings, user_in, uacc_in, item_in, iacc_in,
    users_out, items_out,
    rate, users, uacc, uhalf, gu, items0, vh, term, rs, vsh, bsh,
    load_sem, rs_send, rs_recv, ag_send, ag_recv, sh_send, sh_recv,
):
    me_l, me_g = lax.axis_index("loop"), lax.axis_index("grp")
    nxt, prv = lax.rem(me_l + 1, n_loop), lax.rem(me_l + n_loop - 1, n_loop)
    n_items = item_in.shape[0]
    span = n_items // NC
    piece = span // n_grp
    nb = span // 512
    per = n_grp // nb
    n_blocks = NC * nb

    barrier = pltpu.get_barrier_semaphore()

    def greet(k, _):
        other = lax.rem(me_g + k, n_grp)
        pl.semaphore_signal(barrier, inc=1, device_id=(nxt, other), device_id_type=MESH)
        pl.semaphore_signal(barrier, inc=1, device_id=(prv, other), device_id_type=MESH)

        @pl.when(k > 0)
        def _():
            pl.semaphore_signal(barrier, inc=1, device_id=(me_l, other), device_id_type=MESH)

        return 0

    lax.fori_loop(0, n_grp, greet, 0)

    def row_of(p, owner):
        return pl.multiple_of(p * span + owner * piece, piece)

    loads = [
        pltpu.make_async_copy(user_in, users, load_sem.at[0]),
        pltpu.make_async_copy(item_in, items0, load_sem.at[1]),
        pltpu.make_async_copy(ratings.at[0], rate.at[0], load_sem.at[2]),
        pltpu.make_async_copy(uacc_in, uacc, load_sem.at[3]),
    ]
    for p in range(NC):
        rows = pl.ds(row_of(p, me_g), piece)
        loads.append(pltpu.make_async_copy(iacc_in.at[rows], bsh.at[0, p], load_sem.at[4 + p]))
    loads.append(pltpu.make_async_copy(ratings.at[1], rate.at[1], load_sem.at[4 + NC]))
    for copy in loads:
        copy.start()
    loads[0].wait()
    loads[1].wait()
    uhalf[...] = users[...].astype(jnp.bfloat16)
    vh[0] = items0[...].astype(jnp.bfloat16)
    for p in range(NC):
        vsh[0, p] = items0[pl.ds(row_of(p, me_g), piece)]
    loads[2].wait()
    pl.semaphore_wait(barrier, 3 * n_grp - 1)

    def rs_copy(step, p, owner):
        rows = pl.ds(row_of(p, owner), piece)
        return pltpu.make_async_remote_copy(
            src_ref=term.at[step, rows],
            dst_ref=rs.at[step, p, me_g],
            send_sem=rs_send.at[step, p, owner],
            recv_sem=rs_recv.at[step, p, me_g],
            device_id=(me_l, owner),
            device_id_type=MESH,
        )

    def rs_wait(step, p, source):
        pltpu.make_async_remote_copy(
            src_ref=term.at[step, pl.ds(row_of(p, source), piece)],
            dst_ref=rs.at[step, p, source],
            send_sem=rs_send.at[step, p, source],
            recv_sem=rs_recv.at[step, p, source],
            device_id=(me_l, source),
            device_id_type=MESH,
        ).wait_recv()

    def ag_copy(step, p, worker, member):
        rows = pl.ds(row_of(p, me_g), piece)
        return pltpu.make_async_remote_copy(
            src_ref=vh.at[step + 1, rows],
            dst_ref=vh.at[step + 1, rows],
            send_sem=ag_send.at[step, p, member],
            recv_sem=ag_recv.at[step, p, me_g],
            device_id=(worker, member),
            device_id_type=MESH,
        )

    def ag_wait(step, p, source):
        rows = pl.ds(row_of(p, source), piece)
        pltpu.make_async_remote_copy(
            src_ref=vh.at[step + 1, rows],
            dst_ref=vh.at[step + 1, rows],
            send_sem=ag_send.at[step, p, source],
            recv_sem=ag_recv.at[step, p, source],
            device_id=(me_l, source),
            device_id_type=MESH,
        ).wait_recv()

    def shift_copies(p):
        return [
            pltpu.make_async_remote_copy(
                src_ref=ref.at[1, p],
                dst_ref=ref.at[2, p],
                send_sem=sh_send.at[i, p],
                recv_sem=sh_recv.at[i, p],
                device_id=(nxt, me_g),
                device_id_type=MESH,
            )
            for i, ref in enumerate((vsh, bsh))
        ]

    for step in range(STEPS):
        sub = step // INNER

        def block(j, _, step=step, sub=sub):
            p = j // nb
            b = lax.rem(j % nb + 1 + me_g // per, nb)
            first = pl.multiple_of(p * span + b * 512, 512)
            if step > 0:

                def arrive(q, _):
                    owner = b * per + q
                    if step == INNER:
                        ag_wait(step - 1, p, owner)
                    else:

                        @pl.when(owner != me_g)
                        def _():
                            ag_wait(step - 1, p, owner)

                    return 0

                lax.fori_loop(0, per, arrive, 0)
            user_half = uhalf[...]
            for t in range(2):
                rows = pl.ds(first + t * 256, 256)
                item_half = vh[step, rows]
                predicted = lax.dot_general(
                    user_half, item_half, (((1,), (1,)), ((), ())), preferred_element_type=jnp.float32
                )
                rate_full = rate[sub, :, rows].astype(jnp.float32)
                resid = jnp.where(jnp.abs(rate_full) > 0.25, rate_full - predicted, 0.0).astype(jnp.bfloat16)
                toward = jnp.dot(resid, item_half, preferred_element_type=jnp.float32)
                own = lax.dot_general(
                    resid, user_half, (((0,), (0,)), ((), ())), preferred_element_type=jnp.float32
                )
                term[step, rows] = (-own).astype(jnp.bfloat16)
                gu[...] += toward

            def give(q, _):
                owner = b * per + q

                @pl.when(owner != me_g)
                def _():
                    rs_copy(step, p, owner).start()

                return 0

            lax.fori_loop(0, per, give, 0)
            return 0

        gu[...] = jnp.zeros_like(gu)
        lax.fori_loop(0, n_blocks, block, 0)

        if step == 0:
            loads[3].wait()
            for p in range(NC):
                loads[4 + p].wait()
        if step == INNER - 1:
            loads[4 + NC].wait()
        grad_user = -gu[...] + shrink * users[...]
        new_users, new_acc = adagrad(users[...], uacc[...], grad_user)
        if step < STEPS - 1:
            users[...] = new_users
            uacc[...] = new_acc
            uhalf[...] = new_users.astype(jnp.bfloat16)
        else:
            users_out[...] = new_users

        if step == INNER:
            for p in range(NC):
                for copy in shift_copies(p):
                    copy.wait_recv()

        src, dst = {0: (0, 1), 1: (1, 1), 2: (2, 3), 3: (3, 3)}[step]

        def own_piece(p, _, step=step, src=src, dst=dst):
            rows = pl.ds(row_of(p, me_g), piece)

            def arrive(k, _):
                rs_wait(step, p, lax.rem(me_g + k, n_grp))
                return 0

            lax.fori_loop(1, n_grp, arrive, 0)
            rs[step, p, me_g] = term[step, rows]
            total = rs[step, p, 0].astype(jnp.float32)
            for k in range(1, n_grp):
                total += rs[step, p, k].astype(jnp.float32)
            items = vsh[src, p]
            grad_item = total + shrink * items
            new_items, new_acc = adagrad(items, bsh[src, p], grad_item)
            vsh[dst, p] = new_items
            bsh[dst, p] = new_acc
            if step == STEPS - 1:
                vh[step + 1, rows] = (new_items - vh[step, rows].astype(jnp.float32)).astype(jnp.bfloat16)
            elif step == INNER - 1:
                vh[STEPS + 1, rows] = new_items.astype(jnp.bfloat16)
            else:
                vh[step + 1, rows] = new_items.astype(jnp.bfloat16)

            if step == INNER - 1:

                def send_next(k, _):
                    member = lax.rem(me_g + k, n_grp)
                    pltpu.make_async_remote_copy(
                        src_ref=vh.at[STEPS + 1, rows],
                        dst_ref=vh.at[step + 1, rows],
                        send_sem=ag_send.at[step, p, member],
                        recv_sem=ag_recv.at[step, p, me_g],
                        device_id=(nxt, member),
                        device_id_type=MESH,
                    ).start()
                    return 0

                lax.fori_loop(0, n_grp, send_next, 0)
                for copy in shift_copies(p):
                    copy.start()
            else:

                def send(k, _):
                    ag_copy(step, p, me_l, lax.rem(me_g + k, n_grp)).start()
                    return 0

                lax.fori_loop(1, n_grp, send, 0)
            return 0

        lax.fori_loop(0, NC, own_piece, 0)

    def finish(p, _):
        def arrive(k, _):
            ag_wait(STEPS - 1, p, lax.rem(me_g + k, n_grp))
            return 0

        lax.fori_loop(1, n_grp, arrive, 0)
        rows = pl.ds(pl.multiple_of(p * span, span), span)
        items_out[rows] = vh[STEPS - 1, rows].astype(jnp.float32) + vh[STEPS, rows].astype(jnp.float32)
        return 0

    lax.fori_loop(0, NC, finish, 0)

    for step in range(STEPS):

        def drain(p, _, step=step):
            def one(k, _):
                member = lax.rem(me_g + k, n_grp)
                rs_copy(step, p, member).wait_send()
                ag_copy(step, p, me_l, member).wait_send()
                return 0

            lax.fori_loop(1, n_grp, one, 0)
            if step == INNER - 1:
                ag_copy(step, p, nxt, me_g).wait_send()
                for copy in shift_copies(p):
                    copy.wait_send()
            return 0

        lax.fori_loop(0, NC, drain, 0)


def local(n_loop, n_grp, ratings, user_factors, user_accum, item_factors, item_accum):
    n_users, rank = user_factors.shape
    n_items = item_factors.shape[0]
    piece = n_items // NC // n_grp
    f32, half = jnp.float32, jnp.bfloat16
    sems = pltpu.SemaphoreType.DMA
    return pl.pallas_call(
        functools.partial(kernel, n_loop, n_grp),
        out_shape=(
            jax.ShapeDtypeStruct((n_users, rank), f32),
            jax.ShapeDtypeStruct((n_items, rank), f32),
        ),
        in_specs=[pl.BlockSpec(memory_space=pl.ANY)] * 5,
        out_specs=[pl.BlockSpec(memory_space=pltpu.VMEM)] * 2,
        scratch_shapes=[
            pltpu.VMEM((SUB, n_users, n_items), half),
            pltpu.VMEM((n_users, rank), f32),
            pltpu.VMEM((n_users, rank), f32),
            pltpu.VMEM((n_users, rank), half),
            pltpu.VMEM((n_users, rank), f32),
            pltpu.VMEM((n_items, rank), f32),
            pltpu.VMEM((STEPS + 2, n_items, rank), half),
            pltpu.VMEM((STEPS, n_items, rank), half),
            pltpu.VMEM((STEPS, NC, n_grp, piece, rank), half),
            pltpu.VMEM((4, NC, piece, rank), f32),
            pltpu.VMEM((4, NC, piece, rank), f32),
            sems((5 + NC,)),
            sems((STEPS, NC, n_grp)),
            sems((STEPS, NC, n_grp)),
            sems((STEPS, NC, n_grp)),
            sems((STEPS, NC, n_grp)),
            sems((2, NC)),
            sems((2, NC)),
        ],
        compiler_params=pltpu.CompilerParams(collective_id=0, has_side_effects=True),
        name="epoch",
    )(ratings, user_factors, user_accum, item_factors, item_accum)


def solution(mesh):
    in_specs = (
        P(None, ("loop", "grp"), None),
        P(("loop", "grp"), None),
        P(("loop", "grp"), None),
        P("loop", None),
        P("loop", None),
    )
    out_specs = (P(("loop", "grp"), None), P("loop", None))
    body = functools.partial(local, mesh.shape["loop"], mesh.shape["grp"])
    return jax.shard_map(body, mesh=mesh, in_specs=in_specs, out_specs=out_specs, check_vma=False)
```

time: 460 us -> 83.7 us (0.18)
  the two profiles are of different devices: /device:TPU:64 before, /device:TPU:1 now
where the time goes in v1:
time: 83.7 us; the launch traced here: 83.5 us
  Pallas kernels  79 us (94%)
  local copies, waits for them, and re-layouts  3.93 us (5%)
    pallas_call x1, Pallas kernels, local(): pl.pallas_call(functools.partial(kernel, n_loop, n_grp), out_shape=(jax.S...  79 us
    unnamed x2, local copies, waits for them, and re-layouts  3.93 us

profile of v1, /device:TPU:1, one launch (start us, length us, event | category | flops | bytes accessed | tf_op | source)
XLA Modules:
  0.0 83.5 jit_solution(14280566391940203135)
XLA Ops:
  0.6 79.0 %epoch.1 = (f32[512,128]{1,0:T(8,128)}, f32[2048,128]{1,0:T(8,128)}) custom-call(bf16[2,512,2048]{2,1,0:T(8,128)(2,1)} %ratings.1, f32[512,128]{1,0:T(8,128)} %user_in.1, f32[512,128]{1,0:T(8,128)} %uacc_in.1, f32[2048,128]{1,0:T(8,128)} %item_in.1, f32[2048,128]{1,0:T(8,128)} %iacc_in.1), custom_call_target="tpu_custom_call" | custom-call | tf_op jit(solution)/shard_map/epoch/pallas_call | solution.py:302
  79.6 1.7 %copy.9 = f32[512,128]{1,0:T(8,128)} copy(f32[512,128]{1,0:T(8,128)} %get-tuple-element.4) | data formatting | bytes 524288
  81.3 2.3 %copy.10 = f32[2048,128]{1,0:T(8,128)} copy(f32[2048,128]{1,0:T(8,128)} %get-tuple-element.5) | data formatting | bytes 2097152

commit v2 on v1

v2 whole, which is shorter than its diff:
```python
import functools

import jax
import jax.numpy as jnp
from jax import lax
from jax.experimental import pallas as pl
from jax.experimental.pallas import tpu as pltpu
from jax.sharding import PartitionSpec as P

SUB = 2
INNER = 2
STEPS = SUB * INNER

shrink = 0.05
learn_rate = 0.2
tiny_eps = 1e-06

NC = 8
MESH = pl.DeviceIdType.MESH


def adagrad(param, accum, grad):
    accum = accum + grad * grad
    return param - learn_rate * grad / jnp.sqrt(accum + tiny_eps), accum


def kernel(
    n_loop, n_grp,
    ratings, user_in, uacc_in, item_in, iacc_in,
    users_out, items_out,
    rate, users, uacc, uhalf, gu, items0, vh, term, rs, vsh, bsh,
    load_sem, rs_send, rs_recv, ag_send, ag_recv, sh_send, sh_recv,
):
    me_l, me_g = lax.axis_index("loop"), lax.axis_index("grp")
    nxt, prv = lax.rem(me_l + 1, n_loop), lax.rem(me_l + n_loop - 1, n_loop)
    n_items = item_in.shape[0]
    span = n_items // NC
    piece = span // n_grp

    barrier = pltpu.get_barrier_semaphore()

    def greet(k, _):
        other = lax.rem(me_g + k, n_grp)
        pl.semaphore_signal(barrier, inc=1, device_id=(prv, other), device_id_type=MESH)

        @pl.when(k > 0)
        def _():
            pl.semaphore_signal(barrier, inc=1, device_id=(me_l, other), device_id_type=MESH)

        return 0

    lax.fori_loop(0, n_grp, greet, 0)

    def row_of(p, owner):
        return pl.multiple_of(p * span + owner * piece, piece)

    def load_items(p):
        rows = pl.ds(p * span, span)
        return pltpu.make_async_copy(item_in.at[rows], items0.at[rows], load_sem.at[4 + p])

    def load_rates(p):
        cols = pl.ds(p * span, span)
        return pltpu.make_async_copy(
            ratings.at[0, :, cols], rate.at[0, :, cols], load_sem.at[4 + NC + p]
        )

    def load_accum(p):
        rows = pl.ds(row_of(p, me_g), piece)
        return pltpu.make_async_copy(iacc_in.at[rows], bsh.at[0, p], load_sem.at[4 + 2 * NC + p])

    load_users = pltpu.make_async_copy(user_in, users, load_sem.at[0])
    load_uacc = pltpu.make_async_copy(uacc_in, uacc, load_sem.at[1])
    load_second = pltpu.make_async_copy(ratings.at[1], rate.at[1], load_sem.at[2])
    load_users.start()
    for p in range(NC):
        load_items(p).start()
        load_rates(p).start()
    load_uacc.start()
    for p in range(NC):
        load_accum(p).start()
    load_second.start()
    load_users.wait()
    uhalf[...] = users[...].astype(jnp.bfloat16)
    pl.semaphore_wait(barrier, 2 * n_grp - 1)

    def rs_copy(step, p, owner):
        return pltpu.make_async_remote_copy(
            src_ref=term.at[step, pl.ds(row_of(p, owner), piece)],
            dst_ref=rs.at[step, p, me_g],
            send_sem=rs_send.at[step],
            recv_sem=rs_recv.at[step, p],
            device_id=(me_l, owner),
            device_id_type=MESH,
        )

    def ag_copy(step, p, worker, member, outbox):
        rows = pl.ds(row_of(p, me_g), piece)
        return pltpu.make_async_remote_copy(
            src_ref=vh.at[outbox, rows],
            dst_ref=vh.at[step + 1, rows],
            send_sem=ag_send.at[step],
            recv_sem=ag_recv.at[step, p],
            device_id=(worker, member),
            device_id_type=MESH,
        )

    def await_rows(count, sem):
        rows = pl.ds(0, count)
        pltpu.make_async_copy(term.at[0, rows], term.at[0, rows], sem).wait()

    def shift_copies():
        return [
            pltpu.make_async_remote_copy(
                src_ref=ref.at[1],
                dst_ref=ref.at[2],
                send_sem=sh_send.at[i],
                recv_sem=sh_recv.at[i],
                device_id=(nxt, me_g),
                device_id_type=MESH,
            )
            for i, ref in enumerate((vsh, bsh))
        ]

    for step in range(STEPS):
        sub = step // INNER

        def block(j, _, step=step, sub=sub):
            p = j
            first = pl.multiple_of(p * span, span)
            if step == 0:
                rows = pl.ds(first, span)
                pltpu.make_async_copy(item_in.at[rows], items0.at[rows], load_sem.at[4 + p]).wait()
                pltpu.make_async_copy(
                    ratings.at[0, :, rows], rate.at[0, :, rows], load_sem.at[4 + NC + p]
                ).wait()
                vh[0, rows] = items0[rows].astype(jnp.bfloat16)
                vsh[0, p] = items0[pl.ds(row_of(p, me_g), piece)]
            else:
                senders = n_grp if step == INNER else n_grp - 1
                await_rows(senders * piece, ag_recv.at[step - 1, p])
            user_half = uhalf[...]
            for t in range(span // 256):
                rows = pl.ds(first + t * 256, 256)
                item_half = vh[step, rows]
                predicted = lax.dot_general(
                    user_half, item_half, (((1,), (1,)), ((), ())), preferred_element_type=jnp.float32
                )
                rate_full = rate[sub, :, rows].astype(jnp.float32)
                resid = jnp.where(jnp.abs(rate_full) > 0.25, rate_full - predicted, 0.0).astype(jnp.bfloat16)
                toward = jnp.dot(resid, item_half, preferred_element_type=jnp.float32)
                own = lax.dot_general(
                    resid, user_half, (((0,), (0,)), ((), ())), preferred_element_type=jnp.float32
                )
                term[step, rows] = (-own).astype(jnp.bfloat16)
                gu[...] += toward

            def give(k, _):
                rs_copy(step, p, lax.rem(me_g + k, n_grp)).start()
                return 0

            lax.fori_loop(1, n_grp, give, 0)
            return 0

        gu[...] = jnp.zeros_like(gu)
        lax.fori_loop(0, NC, block, 0)

        if step == 0:
            load_uacc.wait()
            for p in range(NC):
                load_accum(p).wait()
        if step == INNER - 1:
            load_second.wait()
        grad_user = -gu[...] + shrink * users[...]
        new_users, new_acc = adagrad(users[...], uacc[...], grad_user)
        if step < STEPS - 1:
            users[...] = new_users
            uacc[...] = new_acc
            uhalf[...] = new_users.astype(jnp.bfloat16)
        else:
            users_out[...] = new_users

        if step == INNER:
            for copy in shift_copies():
                copy.wait_recv()

        src, dst = {0: (0, 1), 1: (1, 1), 2: (2, 3), 3: (3, 3)}[step]

        def own_piece(p, _, step=step, src=src, dst=dst):
            rows = pl.ds(row_of(p, me_g), piece)

            await_rows((n_grp - 1) * piece, rs_recv.at[step, p])
            rs[step, p, me_g] = term[step, rows]
            total = rs[step, p, 0].astype(jnp.float32)
            for k in range(1, n_grp):
                total += rs[step, p, k].astype(jnp.float32)
            items = vsh[src, p]
            grad_item = total + shrink * items
            new_items, new_acc = adagrad(items, bsh[src, p], grad_item)
            vsh[dst, p] = new_items
            bsh[dst, p] = new_acc
            if step == STEPS - 1:
                vh[step + 1, rows] = (new_items - vh[step, rows].astype(jnp.float32)).astype(jnp.bfloat16)
            elif step == INNER - 1:
                vh[STEPS + 1, rows] = new_items.astype(jnp.bfloat16)
            else:
                vh[step + 1, rows] = new_items.astype(jnp.bfloat16)

            if step == INNER - 1:

                def send(k, _):
                    ag_copy(step, p, nxt, lax.rem(me_g + k, n_grp), STEPS + 1).start()
                    return 0

                lax.fori_loop(0, n_grp, send, 0)
            else:

                def send(k, _):
                    ag_copy(step, p, me_l, lax.rem(me_g + k, n_grp), step + 1).start()
                    return 0

                lax.fori_loop(1, n_grp, send, 0)
            return 0

        lax.fori_loop(0, NC, own_piece, 0)
        if step == INNER - 1:
            for copy in shift_copies():
                copy.start()

    def finish(p, _):
        await_rows((n_grp - 1) * piece, ag_recv.at[STEPS - 1, p])
        rows = pl.ds(pl.multiple_of(p * span, span), span)
        items_out[rows] = vh[STEPS - 1, rows].astype(jnp.float32) + vh[STEPS, rows].astype(jnp.float32)
        return 0

    lax.fori_loop(0, NC, finish, 0)

    for step in range(STEPS):
        await_rows((n_grp - 1) * piece * NC, rs_send.at[step])
        await_rows((n_grp if step == INNER - 1 else n_grp - 1) * piece * NC, ag_send.at[step])
    for copy in shift_copies():
        copy.wait_send()


def local(n_loop, n_grp, ratings, user_factors, user_accum, item_factors, item_accum):
    n_users, rank = user_factors.shape
    n_items = item_factors.shape[0]
    piece = n_items // NC // n_grp
    f32, half = jnp.float32, jnp.bfloat16
    sems = pltpu.SemaphoreType.DMA
    return pl.pallas_call(
        functools.partial(kernel, n_loop, n_grp),
        out_shape=(
            pltpu.VMEM((n_users, rank), f32),
            pltpu.VMEM((n_items, rank), f32),
        ),
        in_specs=[pl.BlockSpec(memory_space=pl.ANY)] * 5,
        out_specs=[pl.BlockSpec(memory_space=pltpu.VMEM)] * 2,
        scratch_shapes=[
            pltpu.VMEM((SUB, n_users, n_items), half),
            pltpu.VMEM((n_users, rank), f32),
            pltpu.VMEM((n_users, rank), f32),
            pltpu.VMEM((n_users, rank), half),
            pltpu.VMEM((n_users, rank), f32),
            pltpu.VMEM((n_items, rank), f32),
            pltpu.VMEM((STEPS + 2, n_items, rank), half),
            pltpu.VMEM((STEPS, n_items, rank), half),
            pltpu.VMEM((STEPS, NC, n_grp, piece, rank), half),
            pltpu.VMEM((4, NC, piece, rank), f32),
            pltpu.VMEM((4, NC, piece, rank), f32),
            sems((4 + 3 * NC,)),
            sems((STEPS,)),
            sems((STEPS, NC)),
            sems((STEPS,)),
            sems((STEPS, NC)),
            sems((2,)),
            sems((2,)),
        ],
        compiler_params=pltpu.CompilerParams(collective_id=0, has_side_effects=True),
        name="epoch",
    )(ratings, user_factors, user_accum, item_factors, item_accum)


def solution(mesh):
    in_specs = (
        P(None, ("loop", "grp"), None),
        P(("loop", "grp"), None),
        P(("loop", "grp"), None),
        P("loop", None),
        P("loop", None),
    )
    out_specs = (P(("loop", "grp"), None), P("loop", None))
    body = functools.partial(local, mesh.shape["loop"], mesh.shape["grp"])
    return jax.shard_map(body, mesh=mesh, in_specs=in_specs, out_specs=out_specs, check_vma=False)
```

time: 83.7 us -> 69.7 us (0.83)
  the two profiles are of different devices: /device:TPU:1 before, /device:TPU:2 now
where the time goes in v2:
time: 69.7 us; the launch traced here: 69.5 us
  Pallas kernels  67.2 us (96%)
  local copies, waits for them, and re-layouts  1.67 us (2%)
    pallas_call x1, Pallas kernels, local(): pl.pallas_call(functools.partial(kernel, n_loop, n_grp), out_shape=(pltpu...  67.2 us
    unnamed x2, local copies, waits for them, and re-layouts  1.67 us

profile of v2, /device:TPU:2, one launch (start us, length us, event | category | flops | bytes accessed | tf_op | source)
XLA Modules:
  0.0 69.5 jit_solution(16967948472021352741)
XLA Ops:
  0.6 67.2 %epoch.1 = (f32[512,128]{1,0:T(8,128)S(1)}, f32[2048,128]{1,0:T(8,128)S(1)}) custom-call(bf16[2,512,2048]{2,1,0:T(8,128)(2,1)} %ratings.1, f32[512,128]{1,0:T(8,128)} %user_in.1, f32[512,128]{1,0:T(8,128)} %uacc_in.1, f32[2048,128]{1,0:T(8,128)} %item_in.1, f32[2048,128]{1,0:T(8,128)} %iacc_in.1), custom_call_target="tpu_custom_call" | custom-call | tf_op jit(solution)/shard_map/epoch/pallas_call | solution.py:250
  67.9 0.7 %copy.9 = f32[512,128]{1,0:T(8,128)} copy(f32[512,128]{1,0:T(8,128)S(1)} %get-tuple-element.2) | data formatting | bytes 524288
  68.6 1.0 %copy.10 = f32[2048,128]{1,0:T(8,128)} copy(f32[2048,128]{1,0:T(8,128)S(1)} %get-tuple-element.3) | data formatting | bytes 2097152

commit v3 on v2

--- a/solution.py
+++ b/solution.py
@@ -16,7 +16,10 @@
 tiny_eps = 1e-06
 
 NC = 8
+AHEAD = NC // 2
 MESH = pl.DeviceIdType.MESH
+
+ORDER = ((2, 1), (2, 0), (1, 1), (3, 1), (1, 0), (3, 0), (0, 1), (0, 0))
 
 
 def adagrad(param, accum, grad):
@@ -51,6 +54,10 @@
 
     lax.fori_loop(0, n_grp, greet, 0)
 
+    def peer(k):
+        dx, dy = ORDER[k]
+        return lax.rem(me_g // 2 + dx, n_grp // 2) * 2 + lax.rem(me_g + dy, 2)
+
     def row_of(p, owner):
         return pl.multiple_of(p * span + owner * piece, piece)
 
@@ -79,6 +86,7 @@
     for p in range(NC):
         load_accum(p).start()
     load_second.start()
+    gu[...] = jnp.zeros_like(gu)
     load_users.wait()
     uhalf[...] = users[...].astype(jnp.bfloat16)
     pl.semaphore_wait(barrier, 2 * n_grp - 1)
@@ -154,14 +162,10 @@
                 term[step, rows] = (-own).astype(jnp.bfloat16)
                 gu[...] += toward
 
-            def give(k, _):
-                rs_copy(step, p, lax.rem(me_g + k, n_grp)).start()
-                return 0
-
-            lax.fori_loop(1, n_grp, give, 0)
+            for k in range(n_grp - 1):
+                rs_copy(step, p, peer(k)).start()
             return 0
 
-        gu[...] = jnp.zeros_like(gu)
         lax.fori_loop(0, NC, block, 0)
 
         if step == 0:
@@ -170,14 +174,16 @@
                 load_accum(p).wait()
         if step == INNER - 1:
             load_second.wait()
-        grad_user = -gu[...] + shrink * users[...]
-        new_users, new_acc = adagrad(users[...], uacc[...], grad_user)
-        if step < STEPS - 1:
-            users[...] = new_users
-            uacc[...] = new_acc
-            uhalf[...] = new_users.astype(jnp.bfloat16)
-        else:
-            users_out[...] = new_users
+        def user_step(step=step):
+            grad_user = -gu[...] + shrink * users[...]
+            new_users, new_acc = adagrad(users[...], uacc[...], grad_user)
+            if step < STEPS - 1:
+                users[...] = new_users
+                uacc[...] = new_acc
+                uhalf[...] = new_users.astype(jnp.bfloat16)
+                gu[...] = jnp.zeros_like(gu)
+            else:
+                users_out[...] = new_users
 
         if step == INNER:
             for copy in shift_copies():
@@ -206,22 +212,16 @@
                 vh[step + 1, rows] = new_items.astype(jnp.bfloat16)
 
             if step == INNER - 1:
-
-                def send(k, _):
-                    ag_copy(step, p, nxt, lax.rem(me_g + k, n_grp), STEPS + 1).start()
-                    return 0
-
-                lax.fori_loop(0, n_grp, send, 0)
+                for k in range(n_grp):
+                    ag_copy(step, p, nxt, peer(k), STEPS + 1).start()
             else:
-
-                def send(k, _):
-                    ag_copy(step, p, me_l, lax.rem(me_g + k, n_grp), step + 1).start()
-                    return 0
-
-                lax.fori_loop(1, n_grp, send, 0)
+                for k in range(n_grp - 1):
+                    ag_copy(step, p, me_l, peer(k), step + 1).start()
             return 0
 
-        lax.fori_loop(0, NC, own_piece, 0)
+        lax.fori_loop(0, AHEAD, own_piece, 0)
+        user_step()
+        lax.fori_loop(AHEAD, NC, own_piece, 0)
         if step == INNER - 1:
             for copy in shift_copies():
                 copy.start()
@@ -239,6 +239,17 @@
         await_rows((n_grp if step == INNER - 1 else n_grp - 1) * piece * NC, ag_send.at[step])
     for copy in shift_copies():
         copy.wait_send()
+
+
+def publish(users, items, users_out, items_out, sem):
+    copies = [
+        pltpu.make_async_copy(items, items_out, sem.at[0]),
+        pltpu.make_async_copy(users, users_out, sem.at[1]),
+    ]
+    for copy in copies:
+        copy.start()
+    for copy in copies:
+        copy.wait()
 
 
 def local(n_loop, n_grp, ratings, user_factors, user_accum, item_factors, item_accum):
@@ -247,7 +258,7 @@
     piece = n_items // NC // n_grp
     f32, half = jnp.float32, jnp.bfloat16
     sems = pltpu.SemaphoreType.DMA
-    return pl.pallas_call(
+    users, items = pl.pallas_call(
         functools.partial(kernel, n_loop, n_grp),
         out_shape=(
             pltpu.VMEM((n_users, rank), f32),
@@ -278,6 +289,17 @@
         compiler_params=pltpu.CompilerParams(collective_id=0, has_side_effects=True),
         name="epoch",
     )(ratings, user_factors, user_accum, item_factors, item_accum)
+    return pl.pallas_call(
+        publish,
+        out_shape=(
+            jax.ShapeDtypeStruct((n_users, rank), f32),
+            jax.ShapeDtypeStruct((n_items, rank), f32),
+        ),
+        in_specs=[pl.BlockSpec(memory_space=pltpu.VMEM)] * 2,
+        out_specs=[pl.BlockSpec(memory_space=pl.ANY)] * 2,
+        scratch_shapes=[sems((2,))],
+        name="publish",
+    )(pltpu.with_memory_space_constraint(users, pltpu.VMEM), pltpu.with_memory_space_constraint(items, pltpu.VMEM))
 
 
 def solution(mesh):

time: 69.7 us -> 68.2 us (0.978)
  local copies, waits for them, and re-layouts: 1.67 us -> 0 us
    unnamed x2 -> x0, local copies, waits for them, and re-layouts: 1.67 us -> none
    pallas_call x0 -> x1, Pallas kernels: none -> 1.07 us  [local(): pl.pallas_call(publish, out_shape=(jax.ShapeDtypeStruct((n_users, rank),...]
    pallas_call x1, Pallas kernels: 67.2 us -> 66.4 us  [local(): pl.pallas_call(functools.partial(kernel, n_loop, n_grp), out_shape=(pltpu...]
where the time goes in v3:
time: 68.2 us; the launch traced here: 68.1 us
  Pallas kernels  67.5 us (99%)
    pallas_call x1, Pallas kernels, local(): pl.pallas_call(functools.partial(kernel, n_loop, n_grp), out_shape=(pltpu...  66.4 us

profile of v3, /device:TPU:2, one launch (start us, length us, event | category | flops | bytes accessed | tf_op | source)
XLA Modules:
  0.0 68.1 jit_solution(14360955244221855338)
XLA Ops:
  0.6 66.4 %epoch.1 = (f32[512,128]{1,0:T(8,128)S(1)}, f32[2048,128]{1,0:T(8,128)S(1)}) custom-call(bf16[2,512,2048]{2,1,0:T(8,128)(2,1)} %ratings.1, f32[512,128]{1,0:T(8,128)} %user_in.1, f32[512,128]{1,0:T(8,128)} %uacc_in.1, f32[2048,128]{1,0:T(8,128)} %item_in.1, f32[2048,128]{1,0:T(8,128)} %iacc_in.1), custom_call_target="tpu_custom_call" | custom-call | tf_op jit(solution)/shard_map/epoch/pallas_call | solution.py:261
  67.0 1.1 %publish.1 = (f32[512,128]{1,0:T(8,128)}, f32[2048,128]{1,0:T(8,128)}) custom-call(f32[512,128]{1,0:T(8,128)S(1)} %get-tuple-element.4.users, f32[2048,128]{1,0:T(8,128)S(1)} %get-tuple-element.5.items), custom_call_target="tpu_custom_call" | custom-call | tf_op jit(solution)/shard_map/publish/pallas_call | solution.py:292
